TPU v7x, 256 devices: a whole 4x4x8 slice. The times are simulated.
256 devices in a mesh: pipe: 16 (over y_hi, z), vocab: 16 (over y_lo, x, core).
Axes of the slice: x: 4, y: 4 (y_hi: 2, y_lo: 2; y = y_hi * 2 + y_lo), z: 8, core: 2. Of those that a mesh axis runs over, the one named last changes fastest.
Arguments:
- final_hidden: bfloat16 [512, 4608], P('pipe', 'vocab'), may hold values from -6 to 6
- tied_table: bfloat16 [163840, 4608], P(('pipe', 'vocab')), may hold values from -1.2 to 1.2
- target_ids: int32 [512], replicated, may hold values from 0 to 163839
- input_ids: int32 [512], replicated, may hold values from 0 to 163839
- embed_cot: bfloat16 [512, 4608], P('pipe', 'vocab'), may hold values from -0.3125 to 0.3125
Outputs:
- grad_table: bfloat16 [163840, 4608], P(('pipe', 'vocab'))
- grad_hidden: float32 [512, 4608], P('pipe', 'vocab')
- token_loss: float32 [512], P('pipe')
All inputs are finite; a program needn't handle non-finite values.
Results may differ from a plain program's by a relative error of at most 0.01.
Values may be sent and summed in bfloat16 or wider, within the bound.
A program may use at most 128 MiB of HBM per device.

v0:
```python
import jax
import jax.numpy as jnp
from jax import lax
from jax.sharding import PartitionSpec as P

D = 4608


def local(final_hidden, tied_table, target_ids, input_ids, embed_cot):
    whole_h, whole_c = (
        lax.all_gather(final_hidden, "vocab", axis=1, tiled=True),
        lax.all_gather(embed_cot, "vocab", axis=1, tiled=True),
    )
    whole_h, whole_c = (
        lax.all_gather(whole_h, "pipe", axis=0, tiled=True),
        lax.all_gather(whole_c, "pipe", axis=0, tiled=True),
    )
    rows_dev = tied_table.shape[0]
    offset = lax.axis_index(("pipe", "vocab")) * rows_dev
    vocab_ids = offset + jnp.arange(rows_dev, dtype=jnp.int32)
    logits = jnp.einsum("td,vd->tv", whole_h, tied_table, preferred_element_type=jnp.float32)
    tanh_part = jnp.tanh(logits / 30.0)
    capped = 30.0 * tanh_part
    exponent = jnp.exp(capped)
    target_mask = vocab_ids[None, :] == target_ids[:, None]
    local_sum = jnp.sum(exponent, axis=1)
    local_target = jnp.sum(jnp.where(target_mask, capped, 0.0), axis=1)
    sum_exp, target_logit = lax.psum((local_sum, local_target), ("pipe", "vocab"))
    token_loss = jnp.log(sum_exp) - target_logit
    dlogits = (
        (exponent / sum_exp[:, None] - target_mask.astype(jnp.float32))
        * (1.0 - tanh_part * tanh_part)
    ).astype(jnp.bfloat16)
    head_grad = jnp.einsum("tv,td->vd", dlogits, whole_h, preferred_element_type=jnp.float32)
    input_mask = (vocab_ids[:, None] == input_ids[None, :]).astype(jnp.bfloat16)
    embed_grad = jnp.dot(input_mask, whole_c, preferred_element_type=jnp.float32)
    grad_table = (head_grad + float(D) ** 0.5 * embed_grad).astype(jnp.bfloat16)
    products = jnp.dot(dlogits, tied_table, preferred_element_type=jnp.float32)
    partial_value = lax.psum_scatter(
        products.astype(jnp.bfloat16), "vocab", scatter_dimension=1, tiled=True
    ).astype(jnp.float32)
    grad_hidden = lax.psum_scatter(partial_value, "pipe", scatter_dimension=0, tiled=True)
    held = final_hidden.shape[0]
    loss_shard = lax.dynamic_slice_in_dim(token_loss, lax.axis_index("pipe") * held, held)
    return (grad_table, grad_hidden, loss_shard)


def solution(mesh):
    placed = (P("pipe", "vocab"), P(("pipe", "vocab"), None), P(), P(), P("pipe", "vocab"))
    return jax.shard_map(
        local,
        mesh=mesh,
        in_specs=placed,
        out_specs=(P(("pipe", "vocab"), None), P("pipe", "vocab"), P("pipe")),
        check_vma=False,
    )
```

profile of v0, /device:TPU:2, one launch (start us, length us, event | category | flops | bytes accessed | tf_op | source)
XLA Modules:
  0.0 609.2 jit_solution(8618035419654364876)
XLA Ops:
  7.2 0.0 all-gather.5.cloned.1.call-start
  7.2 19.4 %all-gather = bf16[16,288,32]{1,2,0:T(8,128)(2,1)S(1)} all-gather(bf16[1,288,32]{1,2,0:T(8,128)(2,1)} %bitcast.20), channel_id=1, replica_groups=mesh['pipe'=16,'vocab'=16] {'vocab'}, dimensions={0}, use_global_device_ids=true | all-gather | bytes 313344 | tf_op jit(solution)/shard_map/all_gather | solution.py:11
  26.7 0.1 copy.12
  26.8 1.1 reshape.18
  27.9 0.0 all-gather.5.cloned.1.call-update
  27.9 0.0 reduce-scatter.5.cloned.1.call-start
  28.0 105.3 %all-gather.5.cloned.1.call-done = bf16[512,4608]{1,0:T(8,128)(2,1)} async-done(((bf16[32,4608]{1,0:T(8,128)(2,1)}), bf16[512,4608]{1,0:T(8,128)(2,1)}) %all-gather.5.cloned.1.call-update) | async-done | bytes 4718608 | tf_op jit(solution)/shard_map/all_gather | solution.py:15
  133.3 7.8 %fusion.4 = (f32[512]{0:T(512)S(1)}, f32[512]{0:T(512)S(1)}, f32[512,640]{1,0:T(8,128)S(1)}) fusion(s32[640]{0:T(1024)S(1)} %iota_add_fusion, s32[512]{0:T(512)S(1)} %copy-done, bf16[512,4608]{1,0:T(8,128)(2,1)} %all-gather.5.cloned.1.call-done, bf16[640,4608]{1,0:T(8,128)(2,1)} %param.6), kind=kOutput, calls=%fused_computation.9 | convolution fusion | flops 3021863936 | bytes 11936256 | tf_op jit(solution)/shard_map/td,vd->tv/dot_general | solution.py:21
  141.0 72.8 %all-reduce = (f32[512]{0:T(512)S(1)}, f32[512]{0:T(512)S(1)}) all-reduce(f32[512]{0:T(512)S(1)} %get-tuple-element.13, f32[512]{0:T(512)S(1)} %get-tuple-element.12), channel_id=1, replica_groups=mesh['pipe'=16,'vocab'=16] {'pipe','vocab'}, use_global_device_ids=true, to_apply=%region_1.2 | all-reduce | flops 1024 | bytes 8192 | tf_op jit(solution)/shard_map/psum | solution.py:28
  213.8 9.8 %convolution_convert_fusion = bf16[512,4608]{0,1:T(8,128)(2,1)} fusion(bf16[640,4608]{1,0:T(8,128)(2,1)} %param.6, f32[512,640]{1,0:T(8,128)S(1)} %get-tuple-element.16, s32[640]{0:T(1024)S(1)} %iota_add_fusion, f32[512]{0:T(512)S(1)} %get-tuple-element.14, s32[512]{0:T(512)S(1)} %copy-done), kind=kOutput, calls=%fused_computation.1 | convolution fusion | flops 3025207296 | bytes 11934208 | tf_op jit(solution)/shard_map/dot_general | solution.py:38
  223.6 0.0 reduce-scatter.5.cloned.1.call-update
  223.6 0.0 all-gather.7.cloned.1.call-start
  223.7 0.7 copy-done.1
  224.4 19.9 %all-gather.1 = bf16[16,288,32]{1,2,0:T(8,128)(2,1)S(1)} all-gather(bf16[1,288,32]{1,2,0:T(8,128)(2,1)S(1)} %bitcast.21), channel_id=1, replica_groups=mesh['pipe'=16,'vocab'=16] {'vocab'}, dimensions={0}, use_global_device_ids=true | all-gather | bytes 313344 | tf_op jit(solution)/shard_map/all_gather | solution.py:12
  244.3 0.1 copy.13
  244.4 1.1 reshape.20
  245.6 0.2 reduce-scatter.7.cloned.1.call-start
  245.8 10.2 %fusion.9 = f32[640,4608]{1,0:T(8,128)} fusion(bf16[512,4608]{1,0:T(8,128)(2,1)} %all-gather.5.cloned.1.call-done, f32[512,640]{1,0:T(8,128)S(1)} %get-tuple-element.16, s32[640]{0:T(1024)S(1)} %iota_add_fusion, f32[512]{0:T(512)S(1)} %get-tuple-element.14, s32[512]{0:T(512)S(1)} %copy-done), kind=kOutput, calls=%fused_computation.16 | convolution fusion | flops 3022848000 | bytes 17832448 | tf_op jit(solution)/shard_map/tv,td->vd/dot_general | solution.py:34
  256.0 32.3 %reduce-scatter.5.cloned.1.call-done = bf16[512,288]{0,1:T(8,128)(2,1)} async-done(((bf16[512,4608]{0,1:T(8,128)(2,1)}), bf16[512,288]{0,1:T(8,128)(2,1)}) %reduce-scatter.5.cloned.1.call-update) | async-done | bytes 294928 | tf_op jit(solution)/shard_map/reduce_scatter | solution.py:39
  288.3 2.0 copy.15
  290.3 0.6 dynamic_slice.3
  290.9 106.2 %all-gather.7.cloned.1.call-done = bf16[512,4608]{1,0:T(8,128)(2,1)} async-done(((bf16[32,4608]{1,0:T(8,128)(2,1)}), bf16[512,4608]{1,0:T(8,128)(2,1)}) %all-gather.7.cloned.1.call-update) | async-done | bytes 4718608 | tf_op jit(solution)/shard_map/all_gather | solution.py:16
  397.1 9.3 %add_convert_fusion = bf16[640,4608]{1,0:T(8,128)(2,1)} fusion(f32[640,4608]{1,0:T(8,128)} %fusion.9, bf16[512,4608]{1,0:T(8,128)(2,1)} %all-gather.7.cloned.1.call-done, s32[512]{0:T(512)S(1)} %copy-done.2, s32[640]{0:T(1024)S(1)} %iota_add_fusion), kind=kOutput, calls=%fused_computation | convolution fusion | flops 3029073920 | bytes 22417920 | tf_op jit(solution)/shard_map/dot_general | solution.py:36
  406.3 196.3 %reduce-scatter.7.cloned.1.call-done = f32[32,288]{1,0:T(8,128)} async-done(((f32[512,288]{1,0:T(8,128)}), f32[32,288]{1,0:T(8,128)}) %reduce-scatter.7.cloned.1.call-update) | async-done | bytes 36880
  (9 shorter events, 0.1 us)
Async XLA Ops:
  7.2 126.1 %copy-start = (s32[512]{0:T(512)S(1)}, s32[512]{0:T(512)}, u32[]{:S(2)}) copy-start(s32[512]{0:T(512)} %param.7) | copy-start | bytes 6148
  7.2 126.1 %all-gather.5.cloned.1.call-start = ((), (), s32[]{:S(2)}) async-start(), calls=%async_computation.2 | async-start | bytes 5013504 | tf_op jit(solution)/shard_map/all_gather | solution.py:15
  27.9 260.3 %reduce-scatter.5.cloned.1.call-start = ((), (), s32[]{:S(2)}) async-start(), calls=%async_computation.4 | async-start | bytes 5013504 | tf_op jit(solution)/shard_map/reduce_scatter | solution.py:39
  223.6 0.7 copy-start.1
  223.6 173.4 %all-gather.7.cloned.1.call-start = ((), (), s32[]{:S(2)}) async-start(), calls=%async_computation.3 | async-start | bytes 5013504 | tf_op jit(solution)/shard_map/all_gather | solution.py:16
  245.6 357.1 %reduce-scatter.7.cloned.1.call-start = ((), (), s32[]{:S(2)}) async-start(), calls=%async_computation.5 | async-start | bytes 835584
  256.0 141.1 %copy-start.2 = (s32[512]{0:T(512)S(1)}, s32[512]{0:T(512)}, u32[]{:S(2)}) copy-start(s32[512]{0:T(512)} %param.8) | copy-start | bytes 6148
Sparse Core Ops, SparseCore 0:
  28.0 105.1 all-gather.4
  223.8 64.4 reduce-scatter.4
  290.9 106.1 all-gather.6
  401.3 201.2 reduce-scatter.6
where the time goes:
time: 610 us; the launch traced here: 609 us
  waiting for transfers between devices  440 us (72%)
  blocking collectives  112 us (18%)
  matrix products  37 us (6%)
  between operations  13.8 us (2%)
    unnamed x5, waiting for transfers between devices  196 us
    all_gather x1, waiting for transfers between devices, local(): lax.all_gather(whole_c, 'pipe', axis=0, tiled=True)  106 us
    all_gather x1, waiting for transfers between devices, local(): lax.all_gather(whole_h, 'pipe', axis=0, tiled=True)  105 us
    psum x1, blocking collectives, local(): lax.psum((local_sum, local_target), ('pipe', 'vocab'))  72.8 us
    reduce_scatter x1, waiting for transfers between devices, local(): lax.psum_scatter(products.astype(jnp.bfloat16), 'vocab', scatter_dimensio...  32.3 us
    all_gather x1, blocking collectives, local(): lax.all_gather(embed_cot, 'vocab', axis=1, tiled=True)  19.9 us
    all_gather x1, blocking collectives, local(): lax.all_gather(final_hidden, 'vocab', axis=1, tiled=True)  19.4 us
  transfers between devices with their start and end apart: 4, of which 4 were waited for; matrix products, arithmetic and copies ran while one was open for 4% of the time, Pallas kernels for 0%

commit v1 on v0

--- a/solution.py
+++ b/solution.py
@@ -11,10 +11,13 @@
         lax.all_gather(final_hidden, "vocab", axis=1, tiled=True),
         lax.all_gather(embed_cot, "vocab", axis=1, tiled=True),
     )
-    whole_h, whole_c = (
-        lax.all_gather(whole_h, "pipe", axis=0, tiled=True),
-        lax.all_gather(whole_c, "pipe", axis=0, tiled=True),
-    )
+
+    def side_run(vals):
+        return jnp.concatenate(
+            jax.lax.all_to_all(jnp.stack([vals] * jax.lax.axis_size("pipe")), "pipe", 0, 0), 0
+        )
+
+    whole_h, whole_c = (side_run(whole_h), lax.all_gather(whole_c, "pipe", axis=0, tiled=True))
     rows_dev = tied_table.shape[0]
     offset = lax.axis_index(("pipe", "vocab")) * rows_dev
     vocab_ids = offset + jnp.arange(rows_dev, dtype=jnp.int32)

time: 610 us -> 579 us (0.949)
  waiting for transfers between devices: 440 us -> 394 us
  starting transfers between devices: 0.35 us -> 10.1 us
    all_to_all x0 -> x1, waiting for transfers between devices: none -> 108 us  [side_run(): jax.lax.all_to_all(jnp.stack([vals] * jax.lax.axis_size('pipe')), 'pipe',...]
    all_gather x1 -> x0, waiting for transfers between devices: 105 us -> none  [local(): lax.all_gather(whole_h, 'pipe', axis=0, tiled=True)]
    all_gather x1, waiting for transfers between devices: 106 us -> 55.3 us  [local(): lax.all_gather(whole_c, 'pipe', axis=0, tiled=True)]
    all_to_all x0 -> x1, starting transfers between devices: none -> 9.84 us  [side_run(): jax.lax.all_to_all(jnp.stack([vals] * jax.lax.axis_size('pipe')), 'pipe',...]
    unnamed x5 -> x4, waiting for transfers between devices: 196 us -> 196 us
where the time goes in v1:
time: 579 us
  waiting for transfers between devices  394 us (68%)
  blocking collectives  114 us (20%)
  matrix products  37 us (6%)
  between operations  15.5 us (3%)
  starting transfers between devices  10.1 us (2%)
  local copies, waits for them, and re-layouts  7.66 us (1%)
    unnamed x4, waiting for transfers between devices  196 us
    all_to_all x1, waiting for transfers between devices, side_run(): jax.lax.all_to_all(jnp.stack([vals] * jax.lax.axis_size('pipe')), 'pipe',...  108 us
    psum x1, blocking collectives, local(): lax.psum((local_sum, local_target), ('pipe', 'vocab'))  75.8 us
    all_gather x1, waiting for transfers between devices, local(): lax.all_gather(whole_c, 'pipe', axis=0, tiled=True)  55.3 us
    reduce_scatter x1, waiting for transfers between devices, local(): lax.psum_scatter(products.astype(jnp.bfloat16), 'vocab', scatter_dimensio...  34 us
    all_gather x1, blocking collectives, local(): lax.all_gather(final_hidden, 'vocab', axis=1, tiled=True)  19.4 us
    all_gather x1, blocking collectives, local(): lax.all_gather(embed_cot, 'vocab', axis=1, tiled=True)  19 us
  transfers between devices with their start and end apart: 4, of which 4 were waited for; matrix products, arithmetic and copies ran while one was open for 4% of the time, Pallas kernels for 0%

profile of v1, /device:TPU:2, one launch (start us, length us, event | category | flops | bytes accessed | tf_op | source)
XLA Modules:
  0.0 578.6 jit_solution(522896226984759603)
XLA Ops:
  8.0 19.4 %all-gather = bf16[16,288,32]{1,2,0:T(8,128)(2,1)S(1)} all-gather(bf16[1,288,32]{1,2,0:T(8,128)(2,1)} %bitcast.21), channel_id=1, replica_groups=mesh['pipe'=16,'vocab'=16] {'vocab'}, dimensions={0}, use_global_device_ids=true | all-gather | bytes 313344 | tf_op jit(solution)/shard_map/all_gather | solution.py:11
  27.4 0.1 copy.13
  27.6 0.4 reshape.24
  28.0 2.6 stack.2
  30.6 9.8 %all-to-all-start = ((bf16[16,32,4608]{2,1,0:T(8,128)(2,1)}), bf16[16,32,4608]{2,1,0:T(8,128)(2,1)}, u32[]{:S(2)}, u32[]{:S(2)}) async-start(bf16[16,32,4608]{2,1,0:T(8,128)(2,1)} %stack.2), calls=%async_computation | async-start | bytes 9437184 | tf_op jit(solution)/shard_map/all_to_all | solution.py:17
  40.4 0.0 reduce-scatter.5.cloned.1.call-start
  40.5 108.4 %all-to-all-done = bf16[16,32,4608]{2,1,0:T(8,128)(2,1)} async-done(((bf16[16,32,4608]{2,1,0:T(8,128)(2,1)}), bf16[16,32,4608]{2,1,0:T(8,128)(2,1)}, u32[]{:S(2)}, u32[]{:S(2)}) %all-to-all-start) | async-done | bytes 4718624 | tf_op jit(solution)/shard_map/all_to_all | solution.py:17
  148.9 7.8 %fusion.4 = (f32[512]{0:T(512)S(1)}, f32[512]{0:T(512)S(1)}, f32[512,640]{1,0:T(8,128)S(1)}) fusion(s32[640]{0:T(1024)S(1)} %iota_add_fusion, s32[512]{0:T(512)S(1)} %copy-done, bf16[512,4608]{1,0:T(8,128)(2,1)} %bitcast.3, bf16[640,4608]{1,0:T(8,128)(2,1)} %param.6), kind=kOutput, calls=%fused_computation.9 | convolution fusion | flops 3021863936 | bytes 11936256 | tf_op jit(solution)/shard_map/td,vd->tv/dot_general | solution.py:24
  156.7 75.8 %all-reduce = (f32[512]{0:T(512)S(1)}, f32[512]{0:T(512)S(1)}) all-reduce(f32[512]{0:T(512)S(1)} %get-tuple-element.13, f32[512]{0:T(512)S(1)} %get-tuple-element.12), channel_id=1, replica_groups=mesh['pipe'=16,'vocab'=16] {'pipe','vocab'}, use_global_device_ids=true, to_apply=%region_1.2 | all-reduce | flops 1024 | bytes 8192 | tf_op jit(solution)/shard_map/psum | solution.py:31
  232.4 9.8 %convolution_convert_fusion = bf16[512,4608]{0,1:T(8,128)(2,1)} fusion(bf16[640,4608]{1,0:T(8,128)(2,1)} %param.6, f32[512,640]{1,0:T(8,128)S(1)} %get-tuple-element.16, s32[640]{0:T(1024)S(1)} %iota_add_fusion, f32[512]{0:T(512)S(1)} %get-tuple-element.14, s32[512]{0:T(512)S(1)} %copy-done), kind=kOutput, calls=%fused_computation.1 | convolution fusion | flops 3025207296 | bytes 11934208 | tf_op jit(solution)/shard_map/dot_general | solution.py:41
  242.2 0.0 all-gather.4.cloned.1.call-start
  242.3 0.7 copy-done.1
  242.9 19.0 %all-gather.1 = bf16[16,288,32]{1,2,0:T(8,128)(2,1)S(1)} all-gather(bf16[1,288,32]{1,2,0:T(8,128)(2,1)S(1)} %bitcast.22), channel_id=1, replica_groups=mesh['pipe'=16,'vocab'=16] {'vocab'}, dimensions={0}, use_global_device_ids=true | all-gather | bytes 313344 | tf_op jit(solution)/shard_map/all_gather | solution.py:12
  261.9 0.1 copy.14
  262.1 1.1 reshape.26
  263.2 0.0 all-gather.4.cloned.1.call-update
  263.2 0.2 reduce-scatter.7.cloned.1.call-start
  263.4 10.2 %fusion.9 = f32[640,4608]{1,0:T(8,128)} fusion(bf16[512,4608]{1,0:T(8,128)(2,1)} %bitcast.3, f32[512,640]{1,0:T(8,128)S(1)} %get-tuple-element.16, s32[640]{0:T(1024)S(1)} %iota_add_fusion, f32[512]{0:T(512)S(1)} %get-tuple-element.14, s32[512]{0:T(512)S(1)} %copy-done), kind=kOutput, calls=%fused_computation.16 | convolution fusion | flops 3022848000 | bytes 17832448 | tf_op jit(solution)/shard_map/tv,td->vd/dot_general | solution.py:37
  273.7 34.0 %reduce-scatter.5.cloned.1.call-done = bf16[512,288]{0,1:T(8,128)(2,1)} async-done(((bf16[512,4608]{0,1:T(8,128)(2,1)}), bf16[512,288]{0,1:T(8,128)(2,1)}) %reduce-scatter.5.cloned.1.call-update) | async-done | bytes 294928 | tf_op jit(solution)/shard_map/reduce_scatter | solution.py:42
  307.6 2.0 copy.16
  309.7 0.6 dynamic_slice.3
  310.3 55.3 %all-gather.4.cloned.1.call-done = bf16[512,4608]{1,0:T(8,128)(2,1)} async-done(((bf16[32,4608]{1,0:T(8,128)(2,1)}), bf16[512,4608]{1,0:T(8,128)(2,1)}) %all-gather.4.cloned.1.call-update) | async-done | bytes 4718608 | tf_op jit(solution)/shard_map/all_gather | solution.py:20
  365.6 9.3 %add_convert_fusion = bf16[640,4608]{1,0:T(8,128)(2,1)} fusion(f32[640,4608]{1,0:T(8,128)} %fusion.9, bf16[512,4608]{1,0:T(8,128)(2,1)} %all-gather.4.cloned.1.call-done, s32[512]{0:T(512)S(1)} %copy-done.2, s32[640]{0:T(1024)S(1)} %iota_add_fusion), kind=kOutput, calls=%fused_computation | convolution fusion | flops 3029073920 | bytes 22417920 | tf_op jit(solution)/shard_map/dot_general | solution.py:39
  374.9 196.3 %reduce-scatter.7.cloned.1.call-done = f32[32,288]{1,0:T(8,128)} async-done(((f32[512,288]{1,0:T(8,128)}), f32[32,288]{1,0:T(8,128)}) %reduce-scatter.7.cloned.1.call-update) | async-done | bytes 36880
  (9 shorter events, 0.1 us)
Async XLA Ops:
  30.6 118.3 %copy-start = (s32[512]{0:T(512)S(1)}, s32[512]{0:T(512)}, u32[]{:S(2)}) copy-start(s32[512]{0:T(512)} %param.7) | copy-start | bytes 6148
  30.6 118.3 %all-to-all-start = ((bf16[16,32,4608]{2,1,0:T(8,128)(2,1)}), bf16[16,32,4608]{2,1,0:T(8,128)(2,1)}, u32[]{:S(2)}, u32[]{:S(2)}) async-start(bf16[16,32,4608]{2,1,0:T(8,128)(2,1)} %stack.2), calls=%async_computation | async-start | bytes 9437184 | tf_op jit(solution)/shard_map/all_to_all | solution.py:17
  40.4 267.2 %reduce-scatter.5.cloned.1.call-start = ((), (), s32[]{:S(2)}) async-start(), calls=%async_computation.4 | async-start | bytes 5013504 | tf_op jit(solution)/shard_map/reduce_scatter | solution.py:42
  242.2 0.7 copy-start.1
  242.2 123.4 %all-gather.4.cloned.1.call-start = ((), (), s32[]{:S(2)}) async-start(), calls=%async_computation.3 | async-start | bytes 5013504 | tf_op jit(solution)/shard_map/all_gather | solution.py:20
  263.2 308.0 %reduce-scatter.7.cloned.1.call-start = ((), (), s32[]{:S(2)}) async-start(), calls=%async_computation.5 | async-start | bytes 835584
  273.7 92.0 %copy-start.2 = (s32[512]{0:T(512)S(1)}, s32[512]{0:T(512)}, u32[]{:S(2)}) copy-start(s32[512]{0:T(512)} %param.8) | copy-start | bytes 6148
Sparse Core Ops, SparseCore 0:
  242.4 65.2 reduce-scatter.4
Sparse Core Ops, SparseCore 1:
  263.3 102.3 all-gather.3
  369.9 201.2 reduce-scatter.6
